TPU v7x, 32 devices: a whole 2x2x4 slice. The times are simulated.
32 devices in a mesh: row: 8 (over y, x, core), col: 4 (over z).
Axes of the slice: x: 2, y: 2, z: 4, core: 2. Of those that a mesh axis runs over, the one named last changes fastest.
Arguments:
- in_map: bfloat16 [128, 128, 256], P('row', 'col'), may hold values from -6 to 6
- tile_w: bfloat16 [3, 3, 256, 256], replicated, may hold values from -0.125 to 0.125
- head_w1: bfloat16 [3, 3, 256, 256], replicated, may hold values from -0.125 to 0.125
- head_w2: bfloat16 [3, 3, 256, 256], replicated, may hold values from -0.125 to 0.125
- box_row: int32 [64, 4], P('row', 'col'), may hold values from 0 to 2
- box_col: int32 [64, 4], P('row', 'col'), may hold values from 0 to 18
- box_target: int32 [64, 4], P('row', 'col'), may hold values from -1 to 15, as said below
- head_cot: bfloat16 [32, 4, 14, 14, 256], P('row', 'col'), may hold values from -6 to 6
Outputs:
- grad_map: bfloat16 [128, 128, 256], P('row', 'col')
- grad_w1: float32 [3, 3, 256, 256], replicated
- grad_w2: float32 [3, 3, 256, 256], replicated
Inputs may be any that keep to these rules, and one draw needn't show every extreme that they name: `box_target`: within each row r of tiles, every head slot d * 4 + h (d below 4, h below 4) is named by exactly one tile slot, and empty slots hold -1. A tile names at most 2 head slots of one device, so it holds at most 8 boxes; in every row of tiles one tile holds 8 boxes, 2 for each device of the row.
All inputs are finite; a program needn't handle non-finite values.
Results may differ from a plain program's by a relative error of at most 0.012.
Values may be sent and summed in bfloat16 or wider, within the bound.
No kernel may reach another device: no remote copies, remote signals or barrier semaphores. Data moves between devices by JAX's collectives and lax.ppermute only.
A program may use at most 64 MiB of HBM per device.

v0:
```python
import math
import jax
import jax.numpy as jnp
from jax import lax
from jax.sharding import PartitionSpec as P

LAYOUT = ("NHWC", "HWIO", "NHWC")


def padded_2(shard, sides, width):
    for axis, dim in sides:
        size, length = (lax.axis_size(axis), shard.shape[dim])
        up = [(i, (i + 1) % size) for i in range(size - 1)]
        down = [(j, i) for i, j in up]
        last = lax.slice_in_dim(shard, length - width, length, axis=dim)
        leading = lax.slice_in_dim(shard, 0, width, axis=dim)
        before = lax.ppermute(last, axis, up)
        after = lax.ppermute(leading, axis, down)
        shard = jnp.concatenate([before, shard, after], axis=dim)
    return shard


def conv_pad(inputs, kernel, margin):
    return lax.conv_general_dilated(
        inputs,
        kernel,
        (1, 1),
        ((margin, margin), (margin, margin)),
        dimension_numbers=LAYOUT,
        preferred_element_type=jnp.float32,
    )


def flip_weights(kernel):
    return jnp.transpose(jnp.flip(kernel, (0, 1)), (0, 1, 3, 2))


def silu_slope(values):
    sigma = jax.nn.sigmoid(values)
    return sigma * (1.0 + values * (1.0 - sigma))


def weight_grad(inputs, deltas):
    channels = inputs.shape[-1]
    box_side = inputs.shape[1]
    padded = jnp.pad(inputs, ((0, 0), (1, 1), (1, 1), (0, 0)))
    flat_delta = deltas.reshape(-1, channels)
    blocks = []
    for shift_y in range(3):
        for shift_x in range(3):
            window = padded[
                :, shift_y : shift_y + box_side, shift_x : shift_x + box_side, :
            ].reshape(-1, channels)
            blocks.append(
                lax.dot_general(
                    window, flat_delta, (((0,), (0,)), ((), ())), preferred_element_type=jnp.float32
                )
            )
    return jnp.stack(blocks).reshape(3, 3, channels, channels)


def pick_rows(table, values):
    flat = values.reshape(values.shape[0], -1)
    return jnp.dot(table, flat, preferred_element_type=jnp.float32).astype(jnp.bfloat16)


def pick_back(table, values):
    return lax.dot_general(
        table, values, (((0,), (0,)), ((), ())), preferred_element_type=jnp.float32
    ).astype(jnp.bfloat16)


def body(in_map, tile_w, head_w1, head_w2, box_row, box_col, box_target, head_cot):
    tile_rows, tile_cols, channels = in_map.shape
    head_count = head_cot.shape[0]
    box_side = head_cot.shape[2]
    slot_count = box_target.shape[0]
    columns = lax.axis_size("col")
    capacity = slot_count // columns
    pair_count = columns * capacity
    padded = padded_2(in_map, (("row", 0), ("col", 1)), 1)
    preact = conv_pad(padded[None], tile_w, 0)[0]
    target = box_target[:, 0]
    occupied = target >= 0
    dest_col = jnp.where(occupied, target // head_count, 0)
    head_slot = jnp.where(occupied, target % head_count, 0)
    slot_ids = jnp.arange(slot_count, dtype=jnp.int32)
    same_dest = (dest_col[:, None] == dest_col[None, :]) & occupied[None, :]
    placing = jnp.sum(same_dest & (slot_ids[None, :] < slot_ids[:, None]), axis=1)
    pair_slot = dest_col * capacity + placing
    pair_ids = jnp.arange(pair_count, dtype=jnp.int32)
    send_map = ((pair_slot[None, :] == pair_ids[:, None]) & occupied[None, :]).astype(jnp.bfloat16)
    head_ids = jnp.arange(head_count, dtype=jnp.int32)
    head_hot = ((head_slot[:, None] == head_ids[None, :]) & occupied[:, None]).astype(jnp.bfloat16)
    pair_head = (
        jnp.dot(send_map, head_hot, preferred_element_type=jnp.float32)
        .astype(jnp.bfloat16)
        .reshape(columns, capacity, head_count)
    )
    top_row = box_row[:, 0]
    left_col = box_col[:, 0]
    zero_index = jnp.zeros((), jnp.int32)
    window = box_side + 2
    windows = jax.vmap(
        lambda y, x: lax.dynamic_slice(padded, (y, x, zero_index), (window, window, channels))
    )(top_row, left_col)
    outgoing = pick_rows(send_map, windows).reshape(columns, capacity, window, window, channels)
    arrived, arrived_head = (
        lax.all_to_all(outgoing, "col", split_axis=0, concat_axis=0, tiled=True),
        lax.all_to_all(pair_head, "col", split_axis=0, concat_axis=0, tiled=True),
    )
    arrived_head = arrived_head.reshape(pair_count, head_count)
    gathered = pick_back(arrived_head, arrived.reshape(pair_count, -1)).reshape(
        head_count, window, window, channels
    )
    box_input = jax.nn.silu(conv_pad(gathered, tile_w, 0)).astype(jnp.bfloat16)
    factor = 1.0 / math.sqrt(lax.axis_size("row") * columns * head_count * box_side * box_side)
    cotangent = head_cot[:, 0]
    pre_one = conv_pad(box_input, head_w1, 1)
    hidden = jax.nn.silu(pre_one).astype(jnp.bfloat16)
    pre_two = conv_pad(hidden, head_w2, 1)
    delta_two = (cotangent.astype(jnp.float32) * silu_slope(pre_two)).astype(jnp.bfloat16)
    second_local = weight_grad(hidden, delta_two)
    delta_one = (conv_pad(delta_two, flip_weights(head_w2), 1) * silu_slope(pre_one)).astype(
        jnp.bfloat16
    )
    box_grads = conv_pad(delta_one, flip_weights(head_w1), 1).astype(jnp.bfloat16)
    sent_back = pick_rows(arrived_head, box_grads).reshape(
        columns, capacity, box_side, box_side, channels
    )
    returned = lax.all_to_all(sent_back, "col", split_axis=0, concat_axis=0, tiled=True)
    slot_grads = pick_back(send_map, returned.reshape(pair_count, -1)).reshape(
        slot_count, box_side, box_side, channels
    )
    first_local = weight_grad(box_input, delta_one)
    first_sum, second_sum = lax.psum((first_local, second_local), ("row", "col"))

    def add_box(slot, running):
        current = lax.dynamic_slice(
            running, (top_row[slot], left_col[slot], zero_index), (box_side, box_side, channels)
        )
        return lax.dynamic_update_slice(
            running,
            current + slot_grads[slot].astype(jnp.float32),
            (top_row[slot], left_col[slot], zero_index),
        )

    box_total = lax.fori_loop(
        0, slot_count, add_box, jnp.zeros((tile_rows, tile_cols, channels), jnp.float32)
    )
    delta_map = (box_total * silu_slope(preact)).astype(jnp.bfloat16)
    delta_rim = padded_2(delta_map, (("row", 0), ("col", 1)), 1)
    grad_map = conv_pad(delta_rim[None], flip_weights(tile_w), 0)[0].astype(jnp.bfloat16)
    return (grad_map, first_sum * factor, second_sum * factor)


def solution(mesh):
    in_specs = (
        P("row", "col", None),
        P(),
        P(),
        P(),
        P("row", "col"),
        P("row", "col"),
        P("row", "col"),
        P("row", "col", None, None, None),
    )
    out_specs = (P("row", "col", None), P(), P())
    return jax.shard_map(body, mesh=mesh, in_specs=in_specs, out_specs=out_specs, check_vma=False)
```

profile of v0, /device:TPU:0, one launch (start us, length us, event | category | flops | bytes accessed | tf_op | source)
XLA Modules:
  0.0 296.8 jit_solution(2329614647910186350)
XLA Ops:
  7.2 0.8 fusion.207
  8.0 1.3 collective-permute-start.1
  9.3 3.0 %collective-permute-start = (bf16[1,32,256]{2,1,0:T(8,128)(2,1)S(1)}, bf16[1,32,256]{2,1,0:T(8,128)(2,1)S(1)}, u32[]{:S(2)}, u32[]{:S(2)}) collective-permute-start(bf16[1,32,256]{2,1,0:T(8,128)(2,1)S(1)} %get-tuple-element.174), channel_id=1, source_target_pairs={{0,4},{4,8},{8,12},{12,16},{16,20},{20,24},{24,28},{1,5},{5,9},{9,... | collective-permute-start | bytes 49160 | tf_op jit(solution)/shard_map/ppermute | solution.py:17
  15.9 1.0 constant_dynamic-update-slice_fusion.1
  16.9 5.0 %collective-permute-start.2 = (bf16[18,1,256]{2,1,0:T(2,128)(2,1)S(1)}, bf16[18,1,256]{2,1,0:T(2,128)(2,1)S(1)}, u32[]{:S(2)}, u32[]{:S(2)}) collective-permute-start(bf16[18,1,256]{2,1,0:T(2,128)(2,1)S(1)} %get-tuple-element.169), channel_id=1, source_target_pairs={{0,1},{1,2},{2,3},{4,5},{5,6},{6,7},{8,9},{9,10},{10,11},{12,13},{... | collective-permute-start | bytes 27656 | tf_op jit(solution)/shard_map/ppermute | solution.py:17
  21.9 1.3 collective-permute-start.3
  23.3 4.3 %collective-permute-done.3 = bf16[18,1,256]{2,1,0:T(2,128)(2,1)S(1)} collective-permute-done((bf16[18,1,256]{2,1,0:T(2,128)(2,1)S(1)}, bf16[18,1,256]{2,1,0:T(2,128)(2,1)S(1)}, u32[]{:S(2)}, u32[]{:S(2)}) %collective-permute-start.3) | collective-permute-done | bytes 9248 | tf_op jit(solution)/shard_map/ppermute | solution.py:18
  27.8 20.0 %while.15 = (s32[]{:T(128)}, bf16[18,34,256]{2,1,0:T(8,128)(2,1)S(1)}, s32[8,3]{0,1:T(4,128)S(1)}, bf16[8,16,16,256]{3,2,1,0:T(8,128)(2,1)}, s32[]{:T(128)}) while((s32[]{:T(128)}, bf16[18,34,256]{2,1,0:T(8,128)(2,1)S(1)}, s32[8,3]{0,1:T(4,128)S(1)}, bf16[8,16,16,256]{3,2,1,0:T(8,128)(2,1)}, s32[]{:T(128)}) %tuple.64), condition=%wide.while_cond, body=%wide.while_body.sunk | while | flops 2 | bytes 263285 | solution.py:105
  28.4 1.9 bitcast_dynamic-update-slice_fusion.2
  30.9 1.9 bitcast_dynamic-update-slice_fusion.2
  33.4 1.9 bitcast_dynamic-update-slice_fusion.2
  35.9 1.9 bitcast_dynamic-update-slice_fusion.2
  38.4 1.9 bitcast_dynamic-update-slice_fusion.2
  40.9 1.9 bitcast_dynamic-update-slice_fusion.2
  43.4 1.9 bitcast_dynamic-update-slice_fusion.2
  45.9 1.9 bitcast_dynamic-update-slice_fusion.2
  47.8 1.8 copy.157
  50.0 1.2 copy.158
  51.2 4.0 %all-to-all-start.1 = ((bf16[4,2,16,16,256]{4,3,2,1,0:T(8,128)(2,1)}), bf16[4,2,16,16,256]{4,3,2,1,0:T(8,128)(2,1)S(1)}, u32[]{:S(2)}, u32[]{:S(2)}) async-start(bf16[4,2,16,16,256]{4,3,2,1,0:T(8,128)(2,1)} %bitcast.140), calls=%async_computation.1 | async-start | bytes 2097152 | tf_op jit(solution)/shard_map/all_to_all | solution.py:109
  56.4 0.9 convolution_select_fusion.3
  57.3 1.1 copy.111
  58.4 22.7 %all-to-all-done.1 = bf16[4,2,16,16,256]{4,3,2,1,0:T(8,128)(2,1)S(1)} async-done(((bf16[4,2,16,16,256]{4,3,2,1,0:T(8,128)(2,1)}), bf16[4,2,16,16,256]{4,3,2,1,0:T(8,128)(2,1)S(1)}, u32[]{:S(2)}, u32[]{:S(2)}) %all-to-all-start.1) | async-done | bytes 1048608 | tf_op jit(solution)/shard_map/all_to_all | solution.py:109
  81.0 3.4 %all-to-all-start = ((bf16[4,2,4]{2,1,0:T(2,128)(2,1)}), bf16[4,2,4]{2,1,0:T(2,128)(2,1)S(1)}, u32[]{:S(2)}, u32[]{:S(2)}) async-start(bf16[4,2,4]{2,1,0:T(2,128)(2,1)} %bitcast.9), calls=%async_computation | async-start | bytes 4096 | tf_op jit(solution)/shard_map/all_to_all | solution.py:110
  84.9 4.8 %all-to-all-done = bf16[4,2,4]{2,1,0:T(2,128)(2,1)S(1)} async-done(((bf16[4,2,4]{2,1,0:T(2,128)(2,1)}), bf16[4,2,4]{2,1,0:T(2,128)(2,1)S(1)}, u32[]{:S(2)}, u32[]{:S(2)}) %all-to-all-start) | async-done | bytes 96 | tf_op jit(solution)/shard_map/all_to_all | solution.py:110
  90.9 1.3 multiply_convert_fusion.1
  93.4 1.2 fusion.43
  94.7 1.1 select_bitcast_fusion.1
  96.4 1.3 add_multiply_fusion
  97.7 0.7 copy.100
  99.1 1.2 fusion.62
  100.3 0.8 copy-done.6
  101.6 2.9 fusion.9
  105.3 0.9 copy_bitcast_fusion.2
  106.2 2.3 copy.120
  108.4 1.2 reshape.164
  109.6 0.8 copy_bitcast_fusion
  110.4 0.9 reshape.174
  111.4 2.5 convolution_convert_fusion.4
  115.5 0.7 reshape.125
  116.3 1.8 copy.105
  118.1 3.5 %all-to-all-start.2 = ((bf16[4,2,14,14,256]{4,1,3,2,0:T(2,128)(2,1)}), bf16[4,2,14,14,256]{4,1,3,2,0:T(2,128)(2,1)S(1)}, u32[]{:S(2)}, u32[]{:S(2)}) async-start(bf16[4,2,14,14,256]{4,1,3,2,0:T(2,128)(2,1)} %copy.105), calls=%async_computation.2 | async-start | bytes 1605632 | tf_op jit(solution)/shard_map/all_to_all | solution.py:131
  121.6 1.4 fusion.28
  128.4 1.0 fusion.19
  129.4 1.0 fusion.18
  130.5 1.1 fusion.17
  131.5 1.0 fusion.16
  132.6 1.0 fusion.15
  134.0 1.3 fusion.14
  135.5 1.1 fusion.13
  136.5 1.1 fusion.12
  137.6 1.1 fusion.11
  138.6 1.8 all-to-all-done.2
  141.9 45.4 %while.14 = (s32[]{:T(128)}, f32[16,32,256]{2,0,1:T(8,128)S(1)}, s32[8]{0:T(128)S(1)}, s32[8]{0:T(128)S(1)}, bf16[8,14,14,256]{3,2,1,0:T(8,128)(2,1)S(1)}, /*index=5*/s32[]{:T(128)}, s32[]{:T(128)}, s32[]{:T(128)}, s32[]{:T(128)}) while((s32[]{:T(128)}, f32[16,32,256]{2,0,1:T(8,128)S(1)}, s32[8]{0:T(128)S(1)}, s32[8]{0:T(128)S(1)}, ...), condition=%wide.region_2.3_spmd, body=%wide.region_1.2_spmd.sunk | while | flops 100360 | bytes 1706193 | solution.py:148
  187.6 1.3 collective-permute-start.4
  188.9 1.3 collective-permute-start.5
  190.2 4.3 %collective-permute-done.5 = bf16[1,32,256]{2,0,1:T(2,128)(2,1)S(1)} collective-permute-done((bf16[1,32,256]{2,0,1:T(2,128)(2,1)S(1)}, bf16[1,32,256]{2,0,1:T(2,128)(2,1)S(1)}, u32[]{:S(2)}, u32[]{:S(2)}) %collective-permute-start.5) | collective-permute-done | bytes 16416 | tf_op jit(solution)/shard_map/ppermute | solution.py:18
  194.6 1.8 collective-permute-start.6
  196.4 1.3 collective-permute-start.7
  197.8 4.2 %collective-permute-done.7 = bf16[18,1,256]{2,0,1:T(8,128)(2,1)S(1)} collective-permute-done((bf16[18,1,256]{2,0,1:T(8,128)(2,1)S(1)}, bf16[18,1,256]{2,0,1:T(8,128)(2,1)S(1)}, u32[]{:S(2)}, u32[]{:S(2)}) %collective-permute-start.7) | collective-permute-done | bytes 9248 | tf_op jit(solution)/shard_map/ppermute | solution.py:18
  202.4 1.0 fusion.10
  203.5 0.8 copy.131
  204.3 80.6 %all-reduce.5.cloned.1.call-done = (f32[3,3,256,256]{3,2,1,0:T(8,128)}, f32[3,3,256,256]{3,2,1,0:T(8,128)}) async-done(((f32[3,3,256,256]{3,2,1,0:T(8,128)}, f32[3,3,256,256]{3,2,1,0:T(8,128)}), (f32[3,3,256,256]{3,2,1,0:T(8,128)}, f32[3,3,256,256]{3,2,1,0:T(8,128)})) %all-reduce.5.cloned.1.call-update) | async-done | bytes 4718608 | tf_op jit(solution)/shard_map/psum | solution.py:136
  284.9 3.4 %broadcast_multiply_fusion.1 = f32[3,3,256,256]{3,2,1,0:T(8,128)} fusion(f32[3,3,256,256]{3,2,1,0:T(8,128)} %get-tuple-element.153), kind=kLoop, calls=%fused_computation.29 | loop fusion | flops 589824 | bytes 4718592 | tf_op jit(solution)/shard_map/mul | solution.py:154
  288.3 1.6 broadcast_multiply_fusion
  (180 shorter events, 39.3 us)
Async XLA Ops:
  7.2 49.2 %copy-start = (bf16[3,3,256,256]{3,2,1,0:T(8,128)(2,1)S(1)}, bf16[3,3,256,256]{3,2,1,0:T(8,128)(2,1)}, u32[]{:S(2)}) copy-start(bf16[3,3,256,256]{3,2,1,0:T(8,128)(2,1)} %param.11) | copy-start | bytes 3538948
  8.0 8.8 %collective-permute-start.1 = (bf16[1,32,256]{2,1,0:T(8,128)(2,1)S(1)}, bf16[1,32,256]{2,1,0:T(8,128)(2,1)S(1)}, u32[]{:S(2)}, u32[]{:S(2)}) collective-permute-start(bf16[1,32,256]{2,1,0:T(8,128)(2,1)S(1)} %get-tuple-element.173), channel_id=1, source_target_pairs={{4,0},{8,4},{12,8},{16,12},{20,16},{24,20},{28,24},{5,1},{9,5},{13... | collective-permute-start | bytes 49160 | tf_op jit(solution)/shard_map/ppermute | solution.py:18
  9.3 6.6 %collective-permute-start = (bf16[1,32,256]{2,1,0:T(8,128)(2,1)S(1)}, bf16[1,32,256]{2,1,0:T(8,128)(2,1)S(1)}, u32[]{:S(2)}, u32[]{:S(2)}) collective-permute-start(bf16[1,32,256]{2,1,0:T(8,128)(2,1)S(1)} %get-tuple-element.174), channel_id=1, source_target_pairs={{0,4},{4,8},{8,12},{12,16},{16,20},{20,24},{24,28},{1,5},{5,9},{9,... | collective-permute-start | bytes 49160 | tf_op jit(solution)/shard_map/ppermute | solution.py:17
  16.9 6.4 %collective-permute-start.2 = (bf16[18,1,256]{2,1,0:T(2,128)(2,1)S(1)}, bf16[18,1,256]{2,1,0:T(2,128)(2,1)S(1)}, u32[]{:S(2)}, u32[]{:S(2)}) collective-permute-start(bf16[18,1,256]{2,1,0:T(2,128)(2,1)S(1)} %get-tuple-element.169), channel_id=1, source_target_pairs={{0,1},{1,2},{2,3},{4,5},{5,6},{6,7},{8,9},{9,10},{10,11},{12,13},{... | collective-permute-start | bytes 27656 | tf_op jit(solution)/shard_map/ppermute | solution.py:17
  21.9 5.7 %collective-permute-start.3 = (bf16[18,1,256]{2,1,0:T(2,128)(2,1)S(1)}, bf16[18,1,256]{2,1,0:T(2,128)(2,1)S(1)}, u32[]{:S(2)}, u32[]{:S(2)}) collective-permute-start(bf16[18,1,256]{2,1,0:T(2,128)(2,1)S(1)} %get-tuple-element.170), channel_id=1, source_target_pairs={{1,0},{2,1},{3,2},{5,4},{6,5},{7,6},{9,8},{10,9},{11,10},{13,12},{... | collective-permute-start | bytes 27656 | tf_op jit(solution)/shard_map/ppermute | solution.py:18
  50.0 5.2 %copy-start.19 = (s32[8,1]{0,1:T(1,128)S(1)}, s32[8,1]{0,1:T(1,128)}, u32[]{:S(2)}) copy-start(s32[8,1]{0,1:T(1,128)} %param.16) | copy-start | bytes 100
  51.2 5.2 %copy-start.20 = (pred[8,5]{0,1:T(8,128)(4,1)S(1)}, pred[8,5]{0,1:T(8,128)(4,1)}, u32[]{:S(2)}) copy-start(pred[8,5]{0,1:T(8,128)(4,1)} %constant.129) | copy-start | bytes 124
  51.2 29.9 %all-to-all-start.1 = ((bf16[4,2,16,16,256]{4,3,2,1,0:T(8,128)(2,1)}), bf16[4,2,16,16,256]{4,3,2,1,0:T(8,128)(2,1)S(1)}, u32[]{:S(2)}, u32[]{:S(2)}) async-start(bf16[4,2,16,16,256]{4,3,2,1,0:T(8,128)(2,1)} %bitcast.140), calls=%async_computation.1 | async-start | bytes 2097152 | tf_op jit(solution)/shard_map/all_to_all | solution.py:109
  81.0 8.7 %all-to-all-start = ((bf16[4,2,4]{2,1,0:T(2,128)(2,1)}), bf16[4,2,4]{2,1,0:T(2,128)(2,1)S(1)}, u32[]{:S(2)}, u32[]{:S(2)}) async-start(bf16[4,2,4]{2,1,0:T(2,128)(2,1)} %bitcast.9), calls=%async_computation | async-start | bytes 4096 | tf_op jit(solution)/shard_map/all_to_all | solution.py:110
  90.2 0.7 copy-start.14
  92.2 1.3 copy-start.18
  94.7 1.2 copy-start.8
  94.7 1.8 copy-start.17
  100.3 0.8 copy-start.6
  105.3 6.1 %copy-start.4 = (bf16[14,4,16,256]{3,2,1,0:T(8,128)(2,1)}, bf16[14,4,16,256]{3,2,1,0:T(8,128)(2,1)S(1)}, u32[]{:S(2)}) copy-start(bf16[14,4,16,256]{3,2,1,0:T(8,128)(2,1)S(1)} %reshape.159) | copy-start | bytes 1376260
  116.3 5.3 %copy-start.10 = (bf16[4,14,14,256]{3,2,1,0:T(8,128)(2,1)S(1)}, bf16[4,14,14,256]{3,2,1,0:T(8,128)(2,1)}, u32[]{:S(2)}) copy-start(bf16[4,14,14,256]{3,2,1,0:T(8,128)(2,1)} %copy_bitcast_fusion.2) | copy-start | bytes 1204228
  118.1 22.3 %all-to-all-start.2 = ((bf16[4,2,14,14,256]{4,1,3,2,0:T(2,128)(2,1)}), bf16[4,2,14,14,256]{4,1,3,2,0:T(2,128)(2,1)S(1)}, u32[]{:S(2)}, u32[]{:S(2)}) async-start(bf16[4,2,14,14,256]{4,1,3,2,0:T(2,128)(2,1)} %copy.105), calls=%async_computation.2 | async-start | bytes 1605632 | tf_op jit(solution)/shard_map/all_to_all | solution.py:131
  121.6 1.5 copy-start.12
  121.6 163.3 %all-reduce.5.cloned.1.call-start = ((), (), s32[]{:S(2)}) async-start(), calls=%async_computation.3 | async-start | bytes 9437184 | tf_op jit(solution)/shard_map/psum | solution.py:136
  123.4 1.0 copy-start.13
  124.5 1.0 copy-start.5
  126.2 1.0 copy-start.11
  127.2 1.0 copy-start.7
  127.2 1.2 copy-start.9
  134.0 1.5 copy-start.2
  140.6 1.3 copy-start.15
  140.6 1.3 copy-start.16
  141.9 45.5 %copy-start.3 = (f32[16,8,5,256]{3,0,2,1:T(8,128)S(1)}, f32[16,8,5,256]{3,0,2,1:T(8,128)}, u32[]{:S(2)}) copy-start(f32[16,8,5,256]{3,0,2,1:T(8,128)} %copy.111) | copy-start | bytes 1966084
  187.6 2.6 collective-permute-start.4
  188.9 5.6 %collective-permute-start.5 = (bf16[1,32,256]{2,0,1:T(2,128)(2,1)S(1)}, bf16[1,32,256]{2,0,1:T(2,128)(2,1)S(1)}, u32[]{:S(2)}, u32[]{:S(2)}) collective-permute-start(bf16[1,32,256]{2,0,1:T(2,128)(2,1)S(1)} %get-tuple-element.172), channel_id=1, source_target_pairs={{4,0},{8,4},{12,8},{16,12},{20,16},{24,20},{28,24},{5,1},{9,5},{13... | collective-permute-start | bytes 49160 | tf_op jit(solution)/shard_map/ppermute | solution.py:18
  194.6 3.2 %collective-permute-start.6 = (bf16[18,1,256]{2,0,1:T(8,128)(2,1)S(1)}, bf16[18,1,256]{2,0,1:T(8,128)(2,1)S(1)}, u32[]{:S(2)}, u32[]{:S(2)}) collective-permute-start(bf16[18,1,256]{2,0,1:T(8,128)(2,1)S(1)} %get-tuple-element.167), channel_id=1, source_target_pairs={{0,1},{1,2},{2,3},{4,5},{5,6},{6,7},{8,9},{9,10},{10,11},{12,13},{... | collective-permute-start | bytes 27656 | tf_op jit(solution)/shard_map/ppermute | solution.py:17
  196.4 5.6 %collective-permute-start.7 = (bf16[18,1,256]{2,0,1:T(8,128)(2,1)S(1)}, bf16[18,1,256]{2,0,1:T(8,128)(2,1)S(1)}, u32[]{:S(2)}, u32[]{:S(2)}) collective-permute-start(bf16[18,1,256]{2,0,1:T(8,128)(2,1)S(1)} %get-tuple-element.168), channel_id=1, source_target_pairs={{1,0},{2,1},{3,2},{5,4},{6,5},{7,6},{9,8},{10,9},{11,10},{13,12},{... | collective-permute-start | bytes 27656 | tf_op jit(solution)/shard_map/ppermute | solution.py:18
  284.9 3.4 %copy-start.1 = (f32[3,3,256,256]{3,2,1,0:T(8,128)S(1)}, f32[3,3,256,256]{3,2,1,0:T(8,128)}, u32[]{:S(2)}) copy-start(f32[3,3,256,256]{3,2,1,0:T(8,128)} %get-tuple-element.154) | copy-start | bytes 7077892
Sparse Core Ops, SparseCore 0:
  138.8 146.0 all-reduce.4
where the time goes:
time: 298 us; the launch traced here: 297 us
  waiting for transfers between devices  123 us (41%)
  local copies, waits for them, and re-layouts  60.4 us (20%)
  loops' own time  31.5 us (11%)
  starting transfers between devices  27.2 us (9%)
  matrix products  27.2 us (9%)
  between operations  14.9 us (5%)
  other arithmetic  12.8 us (4%)
    psum x1, waiting for transfers between devices, body(): lax.psum((first_local, second_local), ('row', 'col'))  80.6 us
    another operation x1, loops' own time, body(): lax.fori_loop(0, slot_count, add_box, jnp.zeros((tile_rows, tile_cols, ch...  31.5 us
    all_to_all x1, waiting for transfers between devices, body(): lax.all_to_all(outgoing, 'col', split_axis=0, concat_axis=0, tiled=True)  22.7 us
    gather x24, local copies, waits for them, and re-layouts  19.9 us
    dot_general x18, matrix products, weight_grad(): lax.dot_general(window, flat_delta, (((0,), (0,)), ((), ())), preferred_e...  14 us
    ppermute x4, waiting for transfers between devices, padded_2(): after = lax.ppermute(leading, axis, down)  12.8 us
    ppermute x4, starting transfers between devices, padded_2(): before = lax.ppermute(last, axis, up)  11.1 us
    conv_general_dilated x7, matrix products, conv_pad(): lax.conv_general_dilated(inputs, kernel, (1, 1), ((margin, margin), (marg...  11.1 us
  transfers between devices with their start and end apart: 12, of which 9 were waited for; matrix products, arithmetic and copies ran while one was open for 13% of the time, Pallas kernels for 0%

commit v1 on v0

--- a/solution.py
+++ b/solution.py
@@ -133,7 +133,7 @@
         slot_count, box_side, box_side, channels
     )
     first_local = weight_grad(box_input, delta_one)
-    first_sum, second_sum = lax.psum((first_local, second_local), ("row", "col"))
+    first_sum, second_sum = lax.psum(lax.psum((first_local, second_local), "col"), "row")
 
     def add_box(slot, running):
         current = lax.dynamic_slice(

time: 298 us -> 408 us (1.37)
  waiting for transfers between devices: 123 us -> 242 us
  local copies, waits for them, and re-layouts: 60.4 us -> 50.2 us
    psum x1 -> x2, waiting for transfers between devices: 80.6 us -> 160 us  [the longest x1 133 us: body(): lax.psum((first_local, second_local), 'col')]
    all_to_all x1, waiting for transfers between devices: 1.77 us -> 40 us  [body(): lax.all_to_all(sent_back, 'col', split_axis=0, concat_axis=0, tiled=True)]
    gather x24, local copies, waits for them, and re-layouts: 19.9 us -> 15.5 us
    unnamed x49 -> x55, local copies, waits for them, and re-layouts: 9.91 us -> 9.38 us
  transfers between devices with their start and end apart: 12 -> 13, of which waited for: 9 -> 10; matrix products, arithmetic and copies ran while one was open for 13% -> 8% of each run, Pallas kernels for 0% -> 0%
where the time goes in v1:
time: 408 us; the launch traced here: 407 us
  waiting for transfers between devices  242 us (59%)
  local copies, waits for them, and re-layouts  50.2 us (12%)
  loops' own time  31.6 us (8%)
  matrix products  27.9 us (7%)
  starting transfers between devices  27.1 us (7%)
  between operations  14.9 us (4%)
  other arithmetic  12.7 us (3%)
    psum x1, waiting for transfers between devices, body(): lax.psum((first_local, second_local), 'col')  133 us
    all_to_all x1, waiting for transfers between devices, body(): lax.all_to_all(sent_back, 'col', split_axis=0, concat_axis=0, tiled=True)  40 us
    another operation x1, loops' own time, body(): lax.fori_loop(0, slot_count, add_box, jnp.zeros((tile_rows, tile_cols, ch...  31.5 us
    psum x1, waiting for transfers between devices, body(): lax.psum(lax.psum((first_local, second_local), 'col'), 'row')  27 us
    all_to_all x1, waiting for transfers between devices, body(): lax.all_to_all(outgoing, 'col', split_axis=0, concat_axis=0, tiled=True)  24.9 us
    gather x24, local copies, waits for them, and re-layouts  15.5 us
    dot_general x18, matrix products, weight_grad(): lax.dot_general(window, flat_delta, (((0,), (0,)), ((), ())), preferred_e...  13.1 us
    conv_general_dilated x7, matrix products, conv_pad(): lax.conv_general_dilated(inputs, kernel, (1, 1), ((margin, margin), (marg...  12.2 us
  transfers between devices with their start and end apart: 13, of which 10 were waited for; matrix products, arithmetic and copies ran while one was open for 8% of the time, Pallas kernels for 0%

profile of v1, /device:TPU:0, one launch (start us, length us, event | category | flops | bytes accessed | tf_op | source)
XLA Modules:
  0.0 406.7 jit_solution(16923372060400342681)
XLA Ops:
  7.2 0.8 fusion.207
  8.0 1.3 collective-permute-start.1
  9.3 3.0 collective-permute-start
  14.3 0.7 compare_select_fusion
  15.2 0.7 multiply_add_fusion
  15.9 1.0 constant_dynamic-update-slice_fusion.1
  16.9 5.0 %collective-permute-start.2 = (bf16[18,1,256]{2,1,0:T(2,128)(2,1)S(1)}, bf16[18,1,256]{2,1,0:T(2,128)(2,1)S(1)}, u32[]{:S(2)}, u32[]{:S(2)}) collective-permute-start(bf16[18,1,256]{2,1,0:T(2,128)(2,1)S(1)} %get-tuple-element.171), channel_id=1, source_target_pairs={{0,1},{1,2},{2,3},{4,5},{5,6},{6,7},{8,9},{9,10},{10,11},{12,13},{... | collective-permute-start | bytes 27656 | tf_op jit(solution)/shard_map/ppermute | solution.py:17
  21.9 1.3 collective-permute-start.3
  23.3 4.3 %collective-permute-done.3 = bf16[18,1,256]{2,1,0:T(2,128)(2,1)S(1)} collective-permute-done((bf16[18,1,256]{2,1,0:T(2,128)(2,1)S(1)}, bf16[18,1,256]{2,1,0:T(2,128)(2,1)S(1)}, u32[]{:S(2)}, u32[]{:S(2)}) %collective-permute-start.3) | collective-permute-done | bytes 9248 | tf_op jit(solution)/shard_map/ppermute | solution.py:18
  27.6 0.9 fusion.200
  28.5 15.7 %while.15 = (s32[]{:T(128)}, bf16[18,34,256]{2,1,0:T(8,128)(2,1)S(1)}, s32[8,3]{0,1:T(4,128)S(1)}, bf16[8,16,16,256]{3,2,1,0:T(8,128)(2,1)S(1)}, s32[]{:T(128)}) while((s32[]{:T(128)}, bf16[18,34,256]{2,1,0:T(8,128)(2,1)S(1)}, s32[8,3]{0,1:T(4,128)S(1)}, bf16[8,16,16,256]{3,2,1,0:T(8,128)(2,1)S(1)}, s32[]{:T(128)}) %tuple.64), condition=%wide.while_cond, body=%wide.while_body.sunk | while | flops 2 | bytes 262269 | solution.py:105
  29.1 1.3 bitcast_dynamic-update-slice_fusion.2
  31.1 1.3 bitcast_dynamic-update-slice_fusion.2
  33.0 1.3 bitcast_dynamic-update-slice_fusion.2
  35.0 1.3 bitcast_dynamic-update-slice_fusion.2
  37.0 1.3 bitcast_dynamic-update-slice_fusion.2
  38.9 1.3 bitcast_dynamic-update-slice_fusion.2
  40.9 1.3 bitcast_dynamic-update-slice_fusion.2
  42.8 1.3 bitcast_dynamic-update-slice_fusion.2
  45.2 1.2 copy.158
  46.4 3.9 all-to-all-start.1
  50.6 0.7 copy.96
  51.2 24.9 %all-to-all-done.1 = bf16[4,2,16,16,256]{4,3,2,1,0:T(8,128)(2,1)S(1)} async-done(((bf16[4,2,16,16,256]{4,3,2,1,0:T(8,128)(2,1)}), bf16[4,2,16,16,256]{4,3,2,1,0:T(8,128)(2,1)S(1)}, u32[]{:S(2)}, u32[]{:S(2)}) %all-to-all-start.1) | async-done | bytes 1048608 | tf_op jit(solution)/shard_map/all_to_all | solution.py:109
  76.1 3.2 all-to-all-start
  80.1 4.7 %all-to-all-done = bf16[4,2,4]{2,1,0:T(2,128)(2,1)S(1)} async-done(((bf16[4,2,4]{2,1,0:T(2,128)(2,1)}), bf16[4,2,4]{2,1,0:T(2,128)(2,1)S(1)}, u32[]{:S(2)}, u32[]{:S(2)}) %all-to-all-start) | async-done | bytes 96 | tf_op jit(solution)/shard_map/all_to_all | solution.py:110
  86.0 1.3 multiply_convert_fusion.1
  88.2 2.6 fusion.43
  92.3 0.9 copy_bitcast_fusion
  93.3 2.6 add_multiply_fusion
  95.9 0.7 copy.100
  97.3 1.2 fusion.62
  98.5 0.7 copy-done.9
  99.8 2.6 fusion.9
  102.4 0.8 copy-done.3
  108.8 1.3 fusion.19
  110.3 1.0 fusion.18
  111.4 1.1 fusion.17
  112.4 1.0 fusion.16
  113.5 1.0 fusion.15
  114.5 1.0 fusion.14
  115.5 1.1 fusion.13
  116.6 1.1 fusion.12
  117.6 1.1 fusion.11
  118.7 1.0 copy-done.4
  120.1 1.3 convolution_convert_fusion.4
  122.7 0.7 reshape.125
  123.5 1.7 copy.105
  125.2 3.6 all-to-all-start.2
  129.2 0.9 convolution_select_fusion.3
  130.3 40.0 %all-to-all-done.2 = bf16[4,2,14,14,256]{4,1,3,2,0:T(2,128)(2,1)S(1)} async-done(((bf16[4,2,14,14,256]{4,1,3,2,0:T(2,128)(2,1)}), bf16[4,2,14,14,256]{4,1,3,2,0:T(2,128)(2,1)S(1)}, u32[]{:S(2)}, u32[]{:S(2)}) %all-to-all-start.2) | async-done | bytes 802848 | tf_op jit(solution)/shard_map/all_to_all | solution.py:131
  171.1 1.1 convolution_convert_fusion.2
  172.3 133.2 %all-reduce.9.cloned.1.call-done = (f32[3,3,256,256]{3,2,1,0:T(8,128)}, f32[3,3,256,256]{3,2,1,0:T(8,128)}) async-done(((f32[3,3,256,256]{3,2,1,0:T(8,128)}, f32[3,3,256,256]{3,2,1,0:T(8,128)}), (f32[3,3,256,256]{3,2,1,0:T(8,128)}, f32[3,3,256,256]{3,2,1,0:T(8,128)})) %all-reduce.9.cloned.1.call-update) | async-done | bytes 4718608 | tf_op jit(solution)/shard_map/psum | solution.py:136
  306.2 45.5 %while.14 = (s32[]{:T(128)}, f32[16,32,256]{2,0,1:T(8,128)S(1)}, s32[8]{0:T(128)S(1)}, s32[8]{0:T(128)S(1)}, bf16[8,14,14,256]{3,2,1,0:T(8,128)(2,1)S(1)}, /*index=5*/s32[]{:T(128)}, s32[]{:T(128)}, s32[]{:T(128)}, s32[]{:T(128)}) while((s32[]{:T(128)}, f32[16,32,256]{2,0,1:T(8,128)S(1)}, s32[8]{0:T(128)S(1)}, s32[8]{0:T(128)S(1)}, ...), condition=%wide.region_2.3_spmd, body=%wide.region_1.2_spmd.sunk | while | flops 100360 | bytes 1706193 | solution.py:148
  352.0 1.6 collective-permute-start.4
  353.6 1.3 collective-permute-start.5
  354.9 3.2 collective-permute-done.5
  358.1 1.4 collective-permute-start.6
  359.5 1.3 collective-permute-start.7
  360.9 4.6 %collective-permute-done.7 = bf16[18,1,256]{2,0,1:T(8,128)(2,1)S(1)} collective-permute-done((bf16[18,1,256]{2,0,1:T(8,128)(2,1)S(1)}, bf16[18,1,256]{2,0,1:T(8,128)(2,1)S(1)}, u32[]{:S(2)}, u32[]{:S(2)}) %collective-permute-start.7) | collective-permute-done | bytes 9248 | tf_op jit(solution)/shard_map/ppermute | solution.py:18
  366.0 1.0 fusion.10
  367.1 0.8 copy.131
  367.8 27.0 %all-reduce.7.cloned.1.call-done = (f32[3,3,256,256]{3,2,1,0:T(8,128)}, f32[3,3,256,256]{3,2,1,0:T(8,128)}) async-done(((f32[3,3,256,256]{3,2,1,0:T(8,128)}, f32[3,3,256,256]{3,2,1,0:T(8,128)}), (f32[3,3,256,256]{3,2,1,0:T(8,128)}, f32[3,3,256,256]{3,2,1,0:T(8,128)})) %all-reduce.7.cloned.1.call-update) | async-done | bytes 4718608 | tf_op jit(solution)/shard_map/psum | solution.py:136
  394.8 3.4 broadcast_multiply_fusion.1
  398.2 1.6 broadcast_multiply_fusion
  (189 shorter events, 38.1 us)
Async XLA Ops:
  7.2 78.7 %copy-start = (bf16[3,3,256,256]{3,2,1,0:T(8,128)(2,1)S(1)}, bf16[3,3,256,256]{3,2,1,0:T(8,128)(2,1)}, u32[]{:S(2)}) copy-start(bf16[3,3,256,256]{3,2,1,0:T(8,128)(2,1)} %param.11) | copy-start | bytes 3538948
  8.0 8.8 %collective-permute-start.1 = (bf16[1,32,256]{2,1,0:T(8,128)(2,1)S(1)}, bf16[1,32,256]{2,1,0:T(8,128)(2,1)S(1)}, u32[]{:S(2)}, u32[]{:S(2)}) collective-permute-start(bf16[1,32,256]{2,1,0:T(8,128)(2,1)S(1)} %get-tuple-element.175), channel_id=1, source_target_pairs={{4,0},{8,4},{12,8},{16,12},{20,16},{24,20},{28,24},{5,1},{9,5},{13... | collective-permute-start | bytes 49160 | tf_op jit(solution)/shard_map/ppermute | solution.py:18
  9.3 6.6 %collective-permute-start = (bf16[1,32,256]{2,1,0:T(8,128)(2,1)S(1)}, bf16[1,32,256]{2,1,0:T(8,128)(2,1)S(1)}, u32[]{:S(2)}, u32[]{:S(2)}) collective-permute-start(bf16[1,32,256]{2,1,0:T(8,128)(2,1)S(1)} %get-tuple-element.176), channel_id=1, source_target_pairs={{0,4},{4,8},{8,12},{12,16},{16,20},{20,24},{24,28},{1,5},{5,9},{9,... | collective-permute-start | bytes 49160 | tf_op jit(solution)/shard_map/ppermute | solution.py:17
  13.0 37.3 %copy-start.16 = (pred[8]{0:T(512)(128)(4,1)}, pred[8]{0:T(512)(128)(4,1)S(1)}, u32[]{:S(2)}) copy-start(pred[8]{0:T(512)(128)(4,1)S(1)} %bitcast_compare_fusion) | copy-start | bytes 28
  15.9 34.4 %copy-start.17 = (s32[8]{0:T(128)}, s32[8]{0:T(128)S(1)}, u32[]{:S(2)}) copy-start(s32[8]{0:T(128)S(1)} %multiply_add_fusion) | copy-start | bytes 100
  16.9 6.4 %collective-permute-start.2 = (bf16[18,1,256]{2,1,0:T(2,128)(2,1)S(1)}, bf16[18,1,256]{2,1,0:T(2,128)(2,1)S(1)}, u32[]{:S(2)}, u32[]{:S(2)}) collective-permute-start(bf16[18,1,256]{2,1,0:T(2,128)(2,1)S(1)} %get-tuple-element.171), channel_id=1, source_target_pairs={{0,1},{1,2},{2,3},{4,5},{5,6},{6,7},{8,9},{9,10},{10,11},{12,13},{... | collective-permute-start | bytes 27656 | tf_op jit(solution)/shard_map/ppermute | solution.py:17
  21.9 5.7 %collective-permute-start.3 = (bf16[18,1,256]{2,1,0:T(2,128)(2,1)S(1)}, bf16[18,1,256]{2,1,0:T(2,128)(2,1)S(1)}, u32[]{:S(2)}, u32[]{:S(2)}) collective-permute-start(bf16[18,1,256]{2,1,0:T(2,128)(2,1)S(1)} %get-tuple-element.172), channel_id=1, source_target_pairs={{1,0},{2,1},{3,2},{5,4},{6,5},{7,6},{9,8},{10,9},{11,10},{13,12},{... | collective-permute-start | bytes 27656 | tf_op jit(solution)/shard_map/ppermute | solution.py:18
  45.2 5.1 %copy-start.21 = (s32[8,1]{0,1:T(1,128)S(1)}, s32[8,1]{0,1:T(1,128)}, u32[]{:S(2)}) copy-start(s32[8,1]{0,1:T(1,128)} %param.16) | copy-start | bytes 100
  46.4 29.7 %all-to-all-start.1 = ((bf16[4,2,16,16,256]{4,3,2,1,0:T(8,128)(2,1)}), bf16[4,2,16,16,256]{4,3,2,1,0:T(8,128)(2,1)S(1)}, u32[]{:S(2)}, u32[]{:S(2)}) async-start(bf16[4,2,16,16,256]{4,3,2,1,0:T(8,128)(2,1)} %bitcast.140), calls=%async_computation.1 | async-start | bytes 2097152 | tf_op jit(solution)/shard_map/all_to_all | solution.py:109
  76.1 8.7 %all-to-all-start = ((bf16[4,2,4]{2,1,0:T(2,128)(2,1)}), bf16[4,2,4]{2,1,0:T(2,128)(2,1)S(1)}, u32[]{:S(2)}, u32[]{:S(2)}) async-start(bf16[4,2,4]{2,1,0:T(2,128)(2,1)} %bitcast.9), calls=%async_computation | async-start | bytes 4096 | tf_op jit(solution)/shard_map/all_to_all | solution.py:110
  79.4 226.2 %all-reduce.9.cloned.1.call-start = ((), (), s32[]{:S(2)}) async-start(), calls=%async_computation.4 | async-start | bytes 9437184 | tf_op jit(solution)/shard_map/psum | solution.py:136
  85.3 0.7 copy-start.15
  88.0 2.7 copy-start.7
  90.7 0.9 copy-start.12
  92.3 1.0 copy-start.5
  98.5 0.8 copy-start.9
  98.5 1.3 copy-start.13
  102.4 0.8 copy-start.3
  105.0 1.0 copy-start.8
  107.7 1.0 copy-start.10
  107.7 1.1 copy-start.14
  108.8 1.5 copy-start.2
  112.4 1.0 copy-start.6
  118.7 1.0 copy-start.4
  118.7 1.4 copy-start.20
  122.7 6.2 %copy-start.11 = (bf16[18,1,34,256]{3,2,0,1:T(8,128)(2,1)S(1)}, bf16[18,1,34,256]{3,2,0,1:T(8,128)(2,1)}, u32[]{:S(2)}) copy-start(bf16[18,1,34,256]{3,2,0,1:T(8,128)(2,1)} %get-tuple-element.167) | copy-start | bytes 940036
  125.2 3.9 copy-start.22
  125.2 45.1 %all-to-all-start.2 = ((bf16[4,2,14,14,256]{4,1,3,2,0:T(2,128)(2,1)}), bf16[4,2,14,14,256]{4,1,3,2,0:T(2,128)(2,1)S(1)}, u32[]{:S(2)}, u32[]{:S(2)}) async-start(bf16[4,2,14,14,256]{4,1,3,2,0:T(2,128)(2,1)} %copy.105), calls=%async_computation.2 | async-start | bytes 1605632 | tf_op jit(solution)/shard_map/all_to_all | solution.py:131
  128.8 265.9 %all-reduce.7.cloned.1.call-start = ((), (), s32[]{:S(2)}) async-start(), calls=%async_computation.3 | async-start | bytes 9437184 | tf_op jit(solution)/shard_map/psum | solution.py:136
  305.6 0.7 copy-start.18
  305.6 0.7 copy-start.19
  351.7 14.3 %copy-start.23 = (pred[8,5]{0,1:T(8,128)(4,1)S(1)}, pred[8,5]{0,1:T(8,128)(4,1)}, u32[]{:S(2)}) copy-start(pred[8,5]{0,1:T(8,128)(4,1)} %constant.129) | copy-start | bytes 124
  352.0 2.9 collective-permute-start.4
  353.6 4.5 %collective-permute-start.5 = (bf16[1,32,256]{2,0,1:T(2,128)(2,1)S(1)}, bf16[1,32,256]{2,0,1:T(2,128)(2,1)S(1)}, u32[]{:S(2)}, u32[]{:S(2)}) collective-permute-start(bf16[1,32,256]{2,0,1:T(2,128)(2,1)S(1)} %get-tuple-element.174), channel_id=1, source_target_pairs={{4,0},{8,4},{12,8},{16,12},{20,16},{24,20},{28,24},{5,1},{9,5},{13... | collective-permute-start | bytes 49160 | tf_op jit(solution)/shard_map/ppermute | solution.py:18
  358.1 2.8 collective-permute-start.6
  359.5 6.0 %collective-permute-start.7 = (bf16[18,1,256]{2,0,1:T(8,128)(2,1)S(1)}, bf16[18,1,256]{2,0,1:T(8,128)(2,1)S(1)}, u32[]{:S(2)}, u32[]{:S(2)}) collective-permute-start(bf16[18,1,256]{2,0,1:T(8,128)(2,1)S(1)} %get-tuple-element.170), channel_id=1, source_target_pairs={{1,0},{2,1},{3,2},{5,4},{6,5},{7,6},{9,8},{10,9},{11,10},{13,12},{... | collective-permute-start | bytes 27656 | tf_op jit(solution)/shard_map/ppermute | solution.py:18
  394.8 3.4 copy-start.1
Sparse Core Ops, SparseCore 0:
  118.8 186.6 all-reduce.8
  308.9 85.8 all-reduce.6
